TPU v7x, 128 devices: a whole 4x4x4 slice. The times are simulated.
128 devices in a mesh: row: 8 (over z, y_lo), col: 16 (over x, y_hi, core).
Axes of the slice: x: 4, y: 4 (y_hi: 2, y_lo: 2; y = y_hi * 2 + y_lo), z: 4, core: 2. Of those that a mesh axis runs over, the one named last changes fastest.
Arguments:
- integrals: bfloat16 [10240, 10240], P('row', 'col'), may hold values from -6 to 6
- amplitudes: bfloat16 [10240, 8192], P('row', 'col'), may hold values from -0.0625 to 0.0625
- int_shape: int32 [40, 40], P('row'), may hold values 0 or 1
- amp_shape: int32 [40, 32], P(None, 'col'), may hold values 0 or 1
Outputs:
- ladder: bfloat16 [10240, 8192], P('row', 'col')
All inputs are finite; a program needn't handle non-finite values. No bound on the sum of `int_shape` or of `amp_shape` on one device may be relied on, other than what follows from the above.
Results may differ from a plain program's by a relative error of at most 0.001.
Values may be sent and summed in bfloat16 or wider, within the bound.
No kernel may reach another device: no remote copies, remote signals or barrier semaphores. Data moves between devices by JAX's collectives and lax.ppermute only.
A program may use at most 192 MiB of HBM per device.

v0:
```python
import jax
import jax.numpy as jnp
from jax import lax
from jax.sharding import PartitionSpec as P

TILE = 256


def expand_shape(shape_mask):
    return jnp.repeat(jnp.repeat(shape_mask, TILE, axis=0), TILE, axis=1).astype(jnp.bfloat16)


def per_device(integrals, amplitudes, int_shape, amp_shape):
    int_mask = expand_shape(int_shape)
    amp_mask = expand_shape(amp_shape)
    whole_amp = lax.all_gather(amplitudes, "row", axis=0, tiled=True) * amp_mask
    left = lax.all_gather(integrals, "col", axis=1, tiled=True) * int_mask
    total = jnp.dot(left, whole_amp, preferred_element_type=jnp.float32)
    return total.astype(jnp.bfloat16)


def solution(mesh):
    in_specs = (P("row", "col"), P("row", "col"), P("row", None), P(None, "col"))
    out_specs = P("row", "col")
    return jax.shard_map(
        per_device, mesh=mesh, in_specs=in_specs, out_specs=out_specs, check_vma=False
    )
```

profile of v0, /device:TPU:1, one launch (start us, length us, event | category | flops | bytes accessed | tf_op | source)
XLA Modules:
  0.0 410.5 jit_solution(6335129066689984502)
XLA Ops:
  6.5 0.0 all-gather.5.cloned.1.call-start
  6.5 0.7 all-gather.5.cloned.1.call-update
  7.3 0.0 all-gather.3.cloned.1.call-start
  7.3 0.7 all-gather.3.cloned.1.call-update
  8.0 0.7 convert_element_type.25
  8.7 12.1 %broadcast_in_dim.13 = bf16[1280,40,256]{2,1,0:T(8,128)(2,1)} broadcast(bf16[1280,40]{1,0:T(8,128)(2,1)S(1)} %bitcast.11), dimensions={0,1} | broadcast | bytes 26316800 | tf_op jit(solution)/shard_map/broadcast_in_dim | solution.py:10
  20.8 0.0 copy-start
  20.8 23.5 %copy.6 = bf16[160,8,40,256]{3,1,2,0:T(8,128)(2,1)} copy(bf16[160,8,40,256]{3,2,1,0:T(8,128)(2,1)} %bitcast.6) | data formatting | bytes 52428800
  44.3 0.0 copy-done
  44.3 0.1 copy.5
  44.4 0.3 broadcast_in_dim.14
  44.8 12.5 %broadcast_in_dim.15 = bf16[10240,2,256]{2,1,0:T(2,128)(2,1)S(1)} broadcast(bf16[10240,2]{1,0:T(8,128)(2,1)S(1)} %bitcast.10), dimensions={0,1} | broadcast | bytes 10526720 | tf_op jit(solution)/shard_map/broadcast_in_dim | solution.py:10
  57.3 7.3 %copy.7 = bf16[1280,8,2,256]{3,1,2,0:T(8,128)(2,1)} copy(bf16[1280,8,2,256]{3,2,1,0:T(2,128)(2,1)S(1)} %bitcast.7) | data formatting | bytes 20971520
  64.6 155.3 %all-gather.5.cloned.1.call-done = bf16[10240,512]{1,0:T(8,128)(2,1)} async-done(((bf16[1280,512]{1,0:T(8,128)(2,1)}), bf16[10240,512]{1,0:T(8,128)(2,1)}) %all-gather.5.cloned.1.call-update) | async-done | bytes 10485776 | tf_op jit(solution)/shard_map/all_gather | solution.py:16
  219.9 156.8 %all-gather.3.cloned.1.call-done = bf16[1280,10240]{1,0:T(8,128)(2,1)} async-done(((bf16[1280,640]{1,0:T(8,128)(2,1)}), bf16[1280,10240]{1,0:T(8,128)(2,1)}) %all-gather.3.cloned.1.call-update) | async-done | bytes 26214416 | tf_op jit(solution)/shard_map/all_gather | solution.py:17
  376.7 27.0 %fusion.3 = bf16[1280,512]{1,0:T(8,128)(2,1)} fusion(bf16[10240,512]{1,0:T(8,128)(2,1)} %all-gather.5.cloned.1.call-done, bf16[10240,512]{1,0:T(8,128)(2,1)} %bitcast.9, bf16[1280,10240]{1,0:T(8,128)(2,1)} %all-gather.3.cloned.1.call-done, bf16[1280,10240]{1,0:T(8,128)(2,1)} %bitcast.8), kind=kOutput, calls=%fused_computation.3 | convolution fusion | flops 13440778240 | bytes 74711040 | tf_op jit(solution)/shard_map/dot_general | solution.py:18
  (2 shorter events, 0.1 us)
Async XLA Ops:
  6.5 213.4 %all-gather.5.cloned.1.call-start = ((), (), s32[]{:S(2)}) async-start(), calls=%async_computation.1 | async-start | bytes 11796480 | tf_op jit(solution)/shard_map/all_gather | solution.py:16
  7.3 369.4 %all-gather.3.cloned.1.call-start = ((), (), s32[]{:S(2)}) async-start(), calls=%async_computation | async-start | bytes 27852800 | tf_op jit(solution)/shard_map/all_gather | solution.py:17
  20.8 23.5 %copy-start = (s32[40,2]{0,1:T(2,128)S(1)}, s32[40,2]{0,1:T(2,128)}, u32[]{:S(2)}) copy-start(s32[40,2]{0,1:T(2,128)} %param.7) | copy-start | bytes 964
Sparse Core Ops, SparseCore 0:
  9.0 210.8 all-gather.4
  222.4 154.2 all-gather.2
where the time goes:
time: 411 us
  waiting for transfers between devices  314 us (76%)
  local copies, waits for them, and re-layouts  55.8 us (14%)
  matrix products  27 us (7%)
  between operations  13.4 us (3%)
    all_gather x1, waiting for transfers between devices, per_device(): left = lax.all_gather(integrals, 'col', axis=1, tiled=True) * int_mask  157 us
    all_gather x1, waiting for transfers between devices, per_device(): whole_amp = lax.all_gather(amplitudes, 'row', axis=0, tiled=True) * amp_mask  155 us
    unnamed x4, local copies, waits for them, and re-layouts  30.7 us
    dot_general x1, matrix products, per_device(): total = jnp.dot(left, whole_amp, preferred_element_type=jnp.float32)  27 us
    broadcast_in_dim x2, local copies, waits for them, and re-layouts, expand_shape(): jnp.repeat(jnp.repeat(shape_mask, TILE, axis=0), TILE, axis=1)  24.6 us
  transfers between devices with their start and end apart: 2, of which 2 were waited for; matrix products, arithmetic and copies ran while one was open for 14% of the time, Pallas kernels for 0%

commit v1 on v0

--- a/solution.py
+++ b/solution.py
@@ -4,6 +4,13 @@
 from jax.sharding import PartitionSpec as P
 
 TILE = 256
+
+
+def exchange_gather(value, axis, dim):
+    size = lax.axis_size(axis)
+    tiles = jnp.stack([value for _ in range(size)])
+    tiles = lax.all_to_all(tiles, axis, split_axis=0, concat_axis=0)
+    return jnp.concatenate(tiles, axis=dim)
 
 
 def expand_shape(shape_mask):
@@ -14,7 +21,7 @@
     int_mask = expand_shape(int_shape)
     amp_mask = expand_shape(amp_shape)
     whole_amp = lax.all_gather(amplitudes, "row", axis=0, tiled=True) * amp_mask
-    left = lax.all_gather(integrals, "col", axis=1, tiled=True) * int_mask
+    left = exchange_gather(integrals, "col", 1) * int_mask
     total = jnp.dot(left, whole_amp, preferred_element_type=jnp.float32)
     return total.astype(jnp.bfloat16)
 

time: 411 us -> 537 us (1.31)
  waiting for transfers between devices: 314 us -> 439 us
  local copies, waits for them, and re-layouts: 55.8 us -> 32 us
  other arithmetic: 0.7 us -> 20.5 us
  starting transfers between devices: 0.04 us -> 8.62 us
    all_to_all x0 -> x1, waiting for transfers between devices: none -> 407 us  [exchange_gather(): tiles = lax.all_to_all(tiles, axis, split_axis=0, concat_axis=0)]
    all_gather x1 -> x0, waiting for transfers between devices: 157 us -> none  [per_device(): left = lax.all_gather(integrals, 'col', axis=1, tiled=True) * int_mask]
    all_gather x1, waiting for transfers between devices: 155 us -> 31.3 us  [per_device(): whole_amp = lax.all_gather(amplitudes, 'row', axis=0, tiled=True) * amp_mask]
    unnamed x4 -> x7, local copies, waits for them, and re-layouts: 30.7 us -> 9.97 us
    mul x0 -> x1, other arithmetic: none -> 20.4 us  [per_device(): left = exchange_gather(integrals, 'col', 1) * int_mask]
    broadcast_in_dim x2 -> x1, local copies, waits for them, and re-layouts: 24.6 us -> 12.5 us  [expand_shape(): jnp.repeat(jnp.repeat(shape_mask, TILE, axis=0), TILE, axis=1)]
    another operation x0 -> x1, local copies, waits for them, and re-layouts: none -> 8.87 us  [exchange_gather(): tiles = jnp.stack([value for _ in range(size)])]
    all_to_all x0 -> x1, starting transfers between devices: none -> 8.58 us  [exchange_gather(): tiles = lax.all_to_all(tiles, axis, split_axis=0, concat_axis=0)]
  transfers between devices with their start and end apart: 2 -> 2, of which waited for: 2 -> 2; matrix products, arithmetic and copies ran while one was open for 14% -> 8% of each run, Pallas kernels for 0% -> 0%
where the time goes in v1:
time: 537 us; the launch traced here: 536 us
  waiting for transfers between devices  439 us (82%)
  local copies, waits for them, and re-layouts  32 us (6%)
  matrix products  23 us (4%)
  other arithmetic  20.5 us (4%)
  between operations  13.5 us (3%)
  starting transfers between devices  8.62 us (2%)
    all_to_all x1, waiting for transfers between devices, exchange_gather(): tiles = lax.all_to_all(tiles, axis, split_axis=0, concat_axis=0)  407 us
    all_gather x1, waiting for transfers between devices, per_device(): whole_amp = lax.all_gather(amplitudes, 'row', axis=0, tiled=True) * amp_mask  31.3 us
    dot_general x1, matrix products, per_device(): total = jnp.dot(left, whole_amp, preferred_element_type=jnp.float32)  23 us
    mul x1, other arithmetic, per_device(): left = exchange_gather(integrals, 'col', 1) * int_mask  20.4 us
    broadcast_in_dim x1, local copies, waits for them, and re-layouts, expand_shape(): jnp.repeat(jnp.repeat(shape_mask, TILE, axis=0), TILE, axis=1)  12.5 us
  transfers between devices with their start and end apart: 2, of which 2 were waited for; matrix products, arithmetic and copies ran while one was open for 8% of the time, Pallas kernels for 0%

profile of v1, /device:TPU:1, one launch (start us, length us, event | category | flops | bytes accessed | tf_op | source)
XLA Modules:
  0.0 536.4 jit_solution(15325847779379082286)
XLA Ops:
  6.5 2.7 copy.9
  9.2 8.9 %stack.2 = bf16[16,1280,640]{1,2,0:T(8,128)(2,1)} broadcast(bf16[1280,640]{0,1:T(8,128)(2,1)S(1)} %copy.9), dimensions={1,2} | broadcast | bytes 27852800 | tf_op jit(solution)/shard_map/stack | solution.py:11
  18.1 0.0 copy-start
  18.1 0.0 copy-start.1
  18.1 8.6 %all-to-all-start = ((bf16[16,1280,640]{1,2,0:T(8,128)(2,1)}), bf16[16,1280,640]{1,2,0:T(8,128)(2,1)}, u32[]{:S(2)}, u32[]{:S(2)}) async-start(bf16[16,1280,640]{1,2,0:T(8,128)(2,1)} %stack.2), calls=%async_computation | async-start | bytes 52428800 | tf_op jit(solution)/shard_map/all_to_all | solution.py:12
  26.7 0.0 all-gather.2.cloned.1.call-start
  26.7 0.7 all-gather.2.cloned.1.call-update
  27.4 0.0 copy-done
  27.4 0.1 copy.10
  27.5 0.1 broadcast_in_dim.12
  27.7 0.0 copy-done.1
  27.7 0.1 copy.11
  27.8 0.3 broadcast_in_dim.14
  28.2 12.5 %broadcast_in_dim.15 = bf16[10240,2,256]{2,1,0:T(2,128)(2,1)S(1)} broadcast(bf16[10240,2]{1,0:T(8,128)(2,1)S(1)} %bitcast.16), dimensions={0,1} | broadcast | bytes 10526720 | tf_op jit(solution)/shard_map/broadcast_in_dim | solution.py:17
  40.7 7.2 %copy.13 = bf16[1280,8,2,256]{3,1,2,0:T(8,128)(2,1)} copy(bf16[1280,8,2,256]{3,2,1,0:T(2,128)(2,1)S(1)} %bitcast.14) | data formatting | bytes 20971520
  48.0 406.9 %all-to-all-done = bf16[16,1280,640]{1,2,0:T(8,128)(2,1)} async-done(((bf16[16,1280,640]{1,2,0:T(8,128)(2,1)}), bf16[16,1280,640]{1,2,0:T(8,128)(2,1)}, u32[]{:S(2)}, u32[]{:S(2)}) %all-to-all-start) | async-done | bytes 26214432 | tf_op jit(solution)/shard_map/all_to_all | solution.py:12
  454.8 20.4 %bitcast_multiply_fusion = bf16[1280,10240]{0,1:T(8,128)(2,1)} fusion(bf16[16,1280,640]{1,2,0:T(8,128)(2,1)} %all-to-all-done, bf16[1280,40]{0,1:T(8,128)(2,1)S(1)} %bitcast.18), kind=kLoop, calls=%fused_computation | loop fusion | flops 13107200 | bytes 52531200 | tf_op jit(solution)/shard_map/mul | solution.py:24
  475.3 31.3 %all-gather.2.cloned.1.call-done = bf16[10240,512]{1,0:T(8,128)(2,1)} async-done(((bf16[1280,512]{1,0:T(8,128)(2,1)}), bf16[10240,512]{1,0:T(8,128)(2,1)}) %all-gather.2.cloned.1.call-update) | async-done | bytes 10485776 | tf_op jit(solution)/shard_map/all_gather | solution.py:23
  506.5 23.0 %fusion.2 = bf16[1280,512]{1,0:T(8,128)(2,1)} fusion(bf16[1280,10240]{0,1:T(8,128)(2,1)} %bitcast_multiply_fusion, bf16[10240,512]{1,0:T(8,128)(2,1)} %all-gather.2.cloned.1.call-done, bf16[10240,512]{1,0:T(8,128)(2,1)} %bitcast.15), kind=kOutput, calls=%fused_computation.3 | convolution fusion | flops 13427671040 | bytes 48496640 | tf_op jit(solution)/shard_map/dot_general | solution.py:25
  (3 shorter events, 0.0 us)
Async XLA Ops:
  18.1 9.3 %copy-start = (s32[5,40]{1,0:T(8,128)S(1)}, s32[5,40]{1,0:T(8,128)}, u32[]{:S(2)}) copy-start(s32[5,40]{1,0:T(8,128)} %param.6) | copy-start | bytes 2404
  18.1 9.6 %copy-start.1 = (s32[40,2]{0,1:T(2,128)S(1)}, s32[40,2]{0,1:T(2,128)}, u32[]{:S(2)}) copy-start(s32[40,2]{0,1:T(2,128)} %param.7) | copy-start | bytes 964
  18.1 436.7 %all-to-all-start = ((bf16[16,1280,640]{1,2,0:T(8,128)(2,1)}), bf16[16,1280,640]{1,2,0:T(8,128)(2,1)}, u32[]{:S(2)}, u32[]{:S(2)}) async-start(bf16[16,1280,640]{1,2,0:T(8,128)(2,1)} %stack.2), calls=%async_computation | async-start | bytes 52428800 | tf_op jit(solution)/shard_map/all_to_all | solution.py:12
  26.7 479.8 %all-gather.2.cloned.1.call-start = ((), (), s32[]{:S(2)}) async-start(), calls=%async_computation.1 | async-start | bytes 11796480 | tf_op jit(solution)/shard_map/all_gather | solution.py:23
Sparse Core Ops, SparseCore 0:
  29.2 477.3 all-gather.1
